TPU v7x, 128 devices: a whole 4x4x4 slice. The times are simulated.
128 devices in a mesh: slab: 16 (over x, z_lo, core), sub: 8 (over z_hi, y).
Axes of the slice: x: 4, y: 4, z: 4 (z_hi: 2, z_lo: 2; z = z_hi * 2 + z_lo), core: 2. Of those that a mesh axis runs over, the one named last changes fastest.
Arguments:
- feats: bfloat16 [655360, 128], P(('slab', 'sub')), may hold values from -6 to 6
- coords: bfloat16 [3, 655360], P(None, ('slab', 'sub')), may hold values from 0 to 1, as said below
- serial: int32 [655360], P(('slab', 'sub')), may hold values from 0 to 5119, as said below
- cells: int32 [655360], P(('slab', 'sub')), may hold values from 0 to 262143, as said below
- counts: int32 [128], P(('slab', 'sub')), may hold values from 2 to 5, as said below
- ghosts: int32 [640], P(('slab', 'sub')), may hold values from 0 to 4
- ln1_gain: float32 [128], replicated, may hold values from 0.5 to 1.5
- w_qkv: bfloat16 [128, 384], replicated
- pos_proj: float32 [3, 256], replicated, may hold values from -6 to 6
- w_out: bfloat16 [128, 128], replicated, may hold values from -0.5 to 0.5
- ln2_gain: float32 [128], replicated, may hold values from 0.5 to 1.5
- w_up: bfloat16 [128, 512], replicated, may hold values from -0.5 to 0.5
- w_down: bfloat16 [512, 128], replicated, may hold values from -0.25 to 0.25
Outputs:
- block_out: bfloat16 [655360, 128], P(('slab', 'sub'))
- pooled: float32 [64, 64, 64, 128], P('slab', 'sub')
Inputs may be any that keep to these rules, and one draw needn't show every extreme that they name: `counts`: each device block's number of live patch slots; live slots are the lowest ones. Some block holds 5 and some holds 2. `serial`: within each device block, a permutation of its local rows 0 to 5119 whose first counts[b] * 1024 entries are rows below counts[b] * 1024. `cells`: A particle of block s * 8 + t lies in a cell with x in s * 4 to (s + 1) * 4 - 1 and y in t * 8 to (t + 1) * 8 - 1. `coords`: positions lie inside their particle's cell, in box units.
All inputs are finite; a program needn't handle non-finite values.
Results may differ from a plain program's by a relative error of at most 0.01.
The roundings to bfloat16 on the way count: a program that leaves them out, or rounds other values in their place, can miss the bound.
Values may be sent and summed in bfloat16 or wider, within the bound.
No kernel may reach another device: no remote copies, remote signals or barrier semaphores. Data moves between devices by JAX's collectives and lax.ppermute only.
A program may use at most 128 MiB of HBM per device.

v0:
```python
import functools
import math

import jax
import jax.numpy as jnp
from jax import lax
from jax.experimental import pallas as pl
from jax.experimental.pallas import tpu as pltpu
from jax.sharding import PartitionSpec as P

HEADS = 4
GRID = 64
EPS = 1e-05
CHUNK = 256
SCALE = math.log2(math.e) / math.sqrt(32.0)
F32 = jnp.float32
BF16 = jnp.bfloat16
VMEM_LIMIT = 24 * 1024 * 1024


def dot(a, b, dims):
    return lax.dot_general(a, b, (dims, ((), ())), preferred_element_type=F32)


def normed_rows(values, gain):
    center = values - jnp.mean(values, axis=-1, keepdims=True)
    spread = jnp.mean(center * center, axis=-1, keepdims=True)
    return (center * lax.rsqrt(spread + EPS) * gain).astype(BF16)


def full_weights(w_full, w_qkv, pos_proj):
    width = w_qkv.shape[0]
    pos = pos_proj[...]
    high = pos.astype(BF16).astype(F32)
    rest = pos - high
    middle = rest.astype(BF16).astype(F32)
    low = rest - middle
    blank = jnp.zeros((16 - 9, 2 * width), F32)
    stacked = jnp.concatenate([high, middle, low, blank], axis=0).astype(BF16)
    w_full[0:width, 0 : 3 * width] = w_qkv[...]
    w_full[width : width + 16, 0 : 2 * width] = stacked
    w_full[width : width + 16, 2 * width : 3 * width] = jnp.zeros((16, width), BF16)
    if w_full.shape[0] > width + 16:
        w_full[width + 16 :, 0 : 3 * width] = jnp.zeros((width - 16, 3 * width), BF16)


def build_tables(feats, coords, cells, table, extra, lines):
    table[...] = feats[...].astype(F32)
    cell = cells[...]
    lines[0:3, :] = coords[...].astype(F32)
    lines[3:4, :] = (((cell >> 12) & 3) * 8 + ((cell >> 6) & 7)).astype(F32)
    lines[4:5, :] = (cell & 63).astype(F32)
    lines[5:6, :] = ((cell >> 13) & 1).astype(F32)
    lines[6:8, :] = jnp.zeros_like(lines[6:8, :])
    source = lax.broadcasted_iota(jnp.int32, (8, 128), 0)
    lane = lax.broadcasted_iota(jnp.int32, (8, 128), 1)
    place_spot = jnp.where((lane < 9) & (lane % 3 == source), 1.0, 0.0)
    cell_spot = jnp.where((lane == source + 6) & (source < 6), 1.0, 0.0)
    spot = jnp.where(source < 3, place_spot, cell_spot).astype(BF16)
    extra[...] = dot(lines[...].astype(BF16), spot, ((0,), (0,)))


def pick_rows(first, rows, serial, table, extra, picked, picked_extra):
    def step(block, carry):
        base = pl.multiple_of(block * 16, 16)
        for r in range(16):
            at = serial[first + base + r]
            picked[pl.ds(base + r, 1), :] = table[pl.ds(at, 1), :]
            picked_extra[pl.ds(base + r, 1), :] = extra[pl.ds(at, 1), :]
        return carry

    lax.fori_loop(0, rows // 16, step, 0)


def near_kernel(rows, serial, feats, coords, cells, ordered, aux, face0, face1, table, extra, picked, picked_extra, lines):
    build_tables(feats, coords, cells, table, extra, lines)
    pick_rows(0, rows, serial, table, extra, picked, picked_extra)
    ordered[...] = picked[...].astype(BF16)
    aux[...] = picked_extra[...].astype(BF16)
    row = lax.broadcasted_iota(jnp.int32, (16, 128), 0)
    lane = lax.broadcasted_iota(jnp.int32, (16, 128), 1)
    pick = jnp.where((row == lane) & (row < 9), 1.0, 0.0).astype(BF16)
    patch = rows // 2
    for face, start in ((face0, 0), (face1, patch)):
        face[0:patch, :] = ordered[start : start + patch, :]
        line = dot(pick, aux[start : start + patch, :], ((1,), (1,))).astype(BF16)
        for c in range(patch // 128):
            face[patch + c * 16 : patch + c * 16 + 16, :] = line[:, c * 128 : c * 128 + 128]


def far_kernel(
    first, serial, table, extra, near, near_aux, gain1, w_qkv, pos_proj,
    ordered, query, keys, values, side, cell_lines,
    picked, picked_extra, w_full,
):
    total, width = table.shape
    full_weights(w_full, w_qkv, pos_proj)
    row = lax.broadcasted_iota(jnp.int32, (width, width), 0)
    w_full[0:width, 3 * width :] = jnp.zeros((width, width), BF16)
    w_full[width:, 3 * width :] = jnp.where(row == 11, 1.0, 0.0).astype(BF16)
    pick_rows(first, total - first, serial, table, extra, picked, picked_extra)
    row = lax.broadcasted_iota(jnp.int32, (8, 128), 0)
    lane = lax.broadcasted_iota(jnp.int32, (8, 128), 1)
    pick = jnp.where((row < 3) & (lane == row + 9), 1.0, 0.0).astype(BF16)
    block = 512
    for lower in range(0, total, block):
        span = slice(lower, lower + block)
        if lower < first:
            wide = near[span, :].astype(F32)
            aux = near_aux[span, :]
            ordered[span, :] = near[span, :]
        else:
            wide = picked[lower - first : lower - first + block, :]
            aux = picked_extra[lower - first : lower - first + block, :].astype(BF16)
            ordered[span, :] = wide.astype(BF16)
        normed = normed_rows(wide, gain1[...])
        qkv = dot(jnp.concatenate([normed, aux], axis=1), w_full[...], ((1,), (0,)))
        query[span, :] = qkv[:, :width].astype(BF16)
        keys[span, :] = qkv[:, width : 2 * width].astype(BF16)
        values[span, :] = qkv[:, 2 * width : 3 * width].astype(BF16)
        side[span, :] = qkv[:, 3 * width :].astype(BF16)
        cell_lines[:, span] = dot(pick, aux, ((1,), (1,)))


def gather_near(serial, feats, coords, cells, rows):
    total, width = feats.shape
    patch = rows // 2
    vm = pl.BlockSpec(memory_space=pltpu.VMEM)
    return pl.pallas_call(
        functools.partial(near_kernel, rows),
        in_specs=[pl.BlockSpec(memory_space=pltpu.SMEM), vm, vm, vm],
        out_specs=[vm] * 6,
        out_shape=[jax.ShapeDtypeStruct((rows, width), BF16), jax.ShapeDtypeStruct((rows, 128), BF16)]
        + [jax.ShapeDtypeStruct((patch + patch // 8, width), BF16)] * 2
        + [jax.ShapeDtypeStruct((total, width), F32), jax.ShapeDtypeStruct((total, 128), F32)],
        scratch_shapes=[
            pltpu.VMEM((rows, width), F32),
            pltpu.VMEM((rows, 128), F32),
            pltpu.VMEM((8, total), F32),
        ],
        compiler_params=pltpu.CompilerParams(vmem_limit_bytes=VMEM_LIMIT),
        name="gather_near",
    )(serial, feats, coords, cells)


def gather_far(serial, table, extra, near, near_aux, gain1, w_qkv, pos_proj):
    total, width = table.shape
    first = near.shape[0]
    vm = pl.BlockSpec(memory_space=pltpu.VMEM)
    return pl.pallas_call(
        functools.partial(far_kernel, first),
        in_specs=[pl.BlockSpec(memory_space=pltpu.SMEM)] + [vm] * 7,
        out_specs=[vm] * 6,
        out_shape=[jax.ShapeDtypeStruct((total, width), BF16)] * 5 + [jax.ShapeDtypeStruct((8, total), F32)],
        scratch_shapes=[
            pltpu.VMEM((total - first, width), F32),
            pltpu.VMEM((total - first, 128), F32),
            pltpu.VMEM((2 * width, 4 * width), BF16),
        ],
        compiler_params=pltpu.CompilerParams(vmem_limit_bytes=VMEM_LIMIT),
        name="gather_far",
    )(serial, table, extra, near, near_aux, gain1, w_qkv, pos_proj)


def block_kernel(
    counts, ghosts, ordered, query, own_keys, own_values, side, cell_lines, face1, face2, face3, face4,
    gain1, w_qkv, pos_proj, w_out, gain2, w_up, w_down,
    out, pooled,
    w_full, keys, values, faces, rows_all, sems,
):
    slot = pl.program_id(0)
    patch, width = out.shape
    slots = ghosts.shape[0]
    depth = width // HEADS
    sources = (face1, face2, face3, face4)

    @pl.when(slot == 0)
    def start():
        for j in range(slots):
            for g in range(4):
                @pl.when((j < counts[0]) & (ghosts[j] == g + 1))
                def fetch():
                    pltpu.make_async_copy(sources[g], faces.at[j], sems.at[j]).start()
        full_weights(w_full, w_qkv, pos_proj)
        values[:, width:] = jnp.ones((2 * patch, width), BF16)

    live = slot < counts[0]
    base = pl.multiple_of(slot * patch, patch)

    @pl.when(jnp.logical_not(live))
    def dead():
        out[...] = jnp.zeros_like(out)
        rows_all[pl.ds(base, patch), :] = jnp.zeros((patch, 2 * width), BF16)

    def finish(lower, mixed):
        stream = (
            ordered[lower : lower + CHUNK, :].astype(F32) + dot(mixed.astype(BF16), w_out[...], ((1,), (0,)))
        ).astype(BF16)
        yield
        wide = stream.astype(F32)
        normed2 = normed_rows(wide, gain2[...])
        yield
        inner = jax.nn.gelu(dot(normed2, w_up[...], ((1,), (0,)))).astype(BF16)
        yield
        result = (wide + dot(inner, w_down[...], ((1,), (0,)))).astype(BF16)
        out[lower : lower + CHUNK, :] = result
        upper = side[lower : lower + CHUNK, :] > 0.5
        none = jnp.zeros_like(result)
        rows_all[pl.ds(base + lower, CHUNK), 0:width] = jnp.where(upper, none, result)
        rows_all[pl.ds(base + lower, CHUNK), width:] = jnp.where(upper, result, none)
        yield

    def attend(count):
        lane = lax.broadcasted_iota(jnp.int32, (CHUNK, width), 1)

        def head_scores(unit):
            lower = unit // HEADS * CHUNK
            h = unit % HEADS
            mine = (lane >= h * depth) & (lane < (h + 1) * depth)
            q = query[lower : lower + CHUNK, :]
            return mine, dot(jnp.where(mine, q, jnp.zeros_like(q)), keys[0:count, :], ((1,), (1,)))

        units = patch // CHUNK * HEADS
        tail = iter(())
        ahead = head_scores(0)
        mixed = jnp.zeros((CHUNK, width), F32)
        for unit in range(units):
            mine, scores = ahead
            if unit + 1 < units:
                ahead = head_scores(unit + 1)
            next(tail, None)
            top = jnp.max(scores, axis=-1, keepdims=True)
            weights = jnp.exp2((scores - top) * SCALE).astype(BF16)
            summed = dot(weights, values[0:count, :], ((1,), (0,)))
            mixed = jnp.where(mine, summed[:, :width] / summed[:, width:], mixed)
            if unit % HEADS == HEADS - 1:
                tail = finish(unit // HEADS * CHUNK, mixed)
        for _ in tail:
            pass

    @pl.when(live)
    def work():
        keys[0:patch, :] = own_keys[...]
        values[0:patch, 0:width] = own_values[...]
        ghost = ghosts[slot]

        @pl.when(ghost > 0)
        def with_ghost():
            pltpu.make_async_copy(face1, faces.at[slot], sems.at[slot]).wait()
            there = normed_rows(faces[slot, 0:patch, :].astype(F32), gain1[...])
            line = jnp.concatenate(
                [faces[slot, patch + c * 16 : patch + c * 16 + 16, :] for c in range(patch // 128)],
                axis=1,
            )
            slab_no = lax.axis_index("slab")
            sub_no = lax.axis_index("sub")
            on_x = ghost < 3
            down = (ghost == 1) | (ghost == 3)
            place = jnp.where(on_x, slab_no, sub_no)
            edge = jnp.where(down, 0, jnp.where(on_x, lax.axis_size("slab"), lax.axis_size("sub")) - 1)
            amount = jnp.where(place == edge, jnp.where(down, -1.0, 1.0), 0.0)
            bump = jnp.where(on_x, pos_proj[0:1, width:], pos_proj[1:2, width:]) * amount
            both = dot(there, w_full[0:width, width:], ((1,), (0,)))
            lifted = dot(line, w_full[width : width + 16, width : 2 * width], ((0,), (0,)))
            keys[patch:, :] = (both[:, :width] + (lifted + bump)).astype(BF16)
            values[patch:, 0:width] = both[:, width:].astype(BF16)
            attend(2 * patch)

        @pl.when(ghost == 0)
        def without_ghost():
            attend(patch)

    @pl.when(slot == slots - 1)
    def pool():
        half = pooled.shape[0] // 2
        row_no = lax.broadcasted_iota(jnp.int32, (1, slots * patch), 1)
        column = jnp.where(row_no < counts[0] * patch, cell_lines[0:1, :], -1.0)
        depth_no = cell_lines[1:2, :]
        ids = lax.broadcasted_iota(jnp.int32, (GRID, 1), 0).astype(F32)
        by_column = jnp.where(column == ids[0 : 2 * half // GRID], 1.0, 0.0).astype(BF16)
        by_depth = jnp.where(depth_no == ids, 1.0, 0.0).astype(BF16)
        tally = jnp.maximum(dot(by_depth, by_column, ((1,), (1,))), 1.0)
        lower_cell = (column - cell_lines[2:3, :] * (half // GRID)) * GRID + depth_no
        wide_ids = lax.broadcasted_iota(jnp.int32, (256, 1), 0).astype(F32)
        for c in range(half // 256):
            onehot = jnp.where(lower_cell == wide_ids + c * 256.0, 1.0, 0.0).astype(BF16)
            summed = dot(onehot, rows_all[...], ((1,), (0,)))
            for k in range(256 // GRID):
                part = summed[k * GRID : (k + 1) * GRID]
                for upper in range(2):
                    at = upper * (half // GRID) + c * (256 // GRID) + k
                    mean = part[:, upper * width : (upper + 1) * width] / tally[:, at : at + 1]
                    pooled[at * GRID : (at + 1) * GRID, :] = mean


def run_block(counts, ghosts, ordered, query, own_keys, own_values, side, cell_lines, faces, gain1, w_qkv, pos_proj, w_out, gain2, w_up, w_down, cells_total):
    slots = ghosts.shape[0]
    width = ordered.shape[1]
    patch = ordered.shape[0] // slots
    smem = pl.BlockSpec(memory_space=pltpu.SMEM)
    vm = pl.BlockSpec(memory_space=pltpu.VMEM)
    hbm = pl.BlockSpec(memory_space=pl.ANY)
    part = pl.BlockSpec((patch, width), lambda j: (j, 0))
    return pl.pallas_call(
        block_kernel,
        grid=(slots,),
        in_specs=[smem, smem] + [part] * 5 + [vm] + [hbm] * 4 + [vm] * 7,
        out_specs=[part, pl.BlockSpec((cells_total, width), lambda j: (0, 0))],
        out_shape=[
            jax.ShapeDtypeStruct((slots * patch, width), BF16),
            jax.ShapeDtypeStruct((cells_total, width), F32),
        ],
        scratch_shapes=[
            pltpu.VMEM((width + 16, 3 * width), BF16),
            pltpu.VMEM((2 * patch, width), BF16),
            pltpu.VMEM((2 * patch, 2 * width), BF16),
            pltpu.VMEM((slots,) + faces[0].shape, BF16),
            pltpu.VMEM((slots * patch, 2 * width), BF16),
            pltpu.SemaphoreType.DMA((slots,)),
        ],
        compiler_params=pltpu.CompilerParams(vmem_limit_bytes=VMEM_LIMIT),
        name="patch_block",
    )(counts, ghosts, ordered, query, own_keys, own_values, side, cell_lines, *faces, gain1, w_qkv, pos_proj, w_out, gain2, w_up, w_down)


def per_device(
    feats, coords, serial, cells, counts, ghosts, ln1_gain, w_qkv, pos_proj, w_out, ln2_gain, w_up, w_down
):
    rows_dev, width = feats.shape
    patch = rows_dev // ghosts.shape[0]
    slab_total = lax.axis_size("slab")
    sub_total = lax.axis_size("sub")
    cells2 = cells.reshape(1, rows_dev)
    gain1 = ln1_gain.reshape(1, width)
    near, near_aux, face0, face1, table, extra = gather_near(serial, feats, coords, cells2, 2 * patch)
    own = gather_far(serial, table, extra, near, near_aux, gain1, w_qkv, pos_proj)

    def ring(axis, size):
        up = [(i, (i + 1) % size) for i in range(size)]
        down = [(j, i) for i, j in up]
        return [lax.ppermute(face1, axis, up), lax.ppermute(face0, axis, down)]

    faces = ring("slab", slab_total) + ring("sub", sub_total)
    planes = GRID // slab_total
    lines = GRID // sub_total
    out, pooled = run_block(
        counts, ghosts, *own, faces,
        gain1, w_qkv, pos_proj, w_out, ln2_gain.reshape(1, width), w_up, w_down,
        planes * lines * GRID,
    )
    return out, pooled.reshape(planes, lines, GRID, width)


def solution(mesh):
    rows = P(("slab", "sub"))
    specs = (P(("slab", "sub"), None), P(None, ("slab", "sub")), rows, rows, rows, rows) + (P(),) * 7
    return jax.shard_map(
        per_device,
        mesh=mesh,
        in_specs=specs,
        out_specs=(P(("slab", "sub"), None), P("slab", "sub", None, None)),
        check_vma=False,
    )
```

profile of v0, /device:TPU:120, one launch (start us, length us, event | category | flops | bytes accessed | tf_op | source)
XLA Modules:
  0.0 90.2 jit_solution(10184176933610130721)
XLA Ops:
  0.6 0.0 copy-start.9
  0.6 0.0 copy-start
  0.7 1.3 %copy-done = bf16[5120,128]{1,0:T(8,128)(2,1)S(1)} copy-done((bf16[5120,128]{1,0:T(8,128)(2,1)S(1)}, bf16[5120,128]{1,0:T(8,128)(2,1)}, u32[]{:S(2)}) %copy-start) | copy-done | bytes 1310744
  2.0 0.0 copy-start.4
  2.0 0.7 copy-done.4
  2.7 0.0 copy-start.5
  2.7 0.8 copy-done.5
  3.5 0.7 copy-done.7
  4.2 5.0 %gather_near.1 = (bf16[2048,128]{1,0:T(8,128)(2,1)S(1)}, bf16[2048,128]{1,0:T(8,128)(2,1)S(1)}, bf16[1152,128]{1,0:T(8,128)(2,1)S(1)}, bf16[1152,128]{1,0:T(8,12...) custom-call(s32[5120]{0:T(1024)S(1)} %copy-done.4, bf16[5120,128]{1,0:T(8,128)(2,1)S(1)} %copy-done, ...), custom_call_target="tpu_custom_call" | custom-call | tf_op jit(solution)/shard_map/gather_near/pallas_call | solution.py:129
  9.2 0.1 collective-permute-start
  9.3 1.7 %collective-permute-start.1 = (bf16[1152,128]{1,0:T(8,128)(2,1)S(1)}, bf16[1152,128]{1,0:T(8,128)(2,1)S(1)}, u32[]{:S(2)}, u32[]{:S(2)}) collective-permute-start(bf16[1152,128]{1,0:T(8,128)(2,1)S(1)} %get-tuple-element.27), channel_id=1, source_target_pairs={{8,0},{16,8},{24,16},{32,24},{40,32},{48,40},{56,48},{64,56},{72,6... | collective-permute-start | bytes 884744 | tf_op jit(solution)/shard_map/ppermute | solution.py:341
  11.0 0.2 collective-permute-start.2
  11.2 1.8 %collective-permute-start.3 = (bf16[1152,128]{1,0:T(8,128)(2,1)S(1)}, bf16[1152,128]{1,0:T(8,128)(2,1)S(1)}, u32[]{:S(2)}, u32[]{:S(2)}) collective-permute-start(bf16[1152,128]{1,0:T(8,128)(2,1)S(1)} %get-tuple-element.27), channel_id=1, source_target_pairs={{1,0},{2,1},{3,2},{4,3},{5,4},{6,5},{7,6},{0,7},{9,8},{10,9},{11,1... | collective-permute-start | bytes 884744 | tf_op jit(solution)/shard_map/ppermute | solution.py:341
  13.7 0.0 copy-done.9
  13.7 0.0 copy-done.1
  13.7 0.0 copy-done.8
  13.7 0.0 copy-start.2
  13.7 0.0 copy-start.3
  13.7 0.0 copy-start.6
  13.7 0.0 copy-start.10
  13.7 0.0 copy-start.11
  13.8 9.2 %gather_far.1 = (bf16[5120,128]{1,0:T(8,128)(2,1)S(1)}, bf16[5120,128]{1,0:T(8,128)(2,1)S(1)}, bf16[5120,128]{1,0:T(8,128)(2,1)S(1)}, bf16[5120,128]{1,0:T(8,128...) custom-call(s32[5120]{0:T(1024)S(1)} %copy-done.4, f32[5120,128]{1,0:T(8,128)S(1)} %get-tuple-element.16.table, ...), custom_call_target="tpu_custom_call" | custom-call | tf_op jit(solution)/shard_map/gather_far/pallas_call | solution.py:150
  23.0 1.9 %collective-permute-done.face1 = bf16[1152,128]{1,0:T(8,128)(2,1)S(1)} collective-permute-done((bf16[1152,128]{1,0:T(8,128)(2,1)S(1)}, bf16[1152,128]{1,0:T(8,128)(2,1)S(1)}, u32[]{:S(2)}, u32[]{:S(2)}) %collective-permute-start) | collective-permute-done | bytes 294944 | tf_op jit(solution)/shard_map/ppermute | solution.py:341
  24.9 0.0 collective-permute-done.1.face2
  24.9 0.0 collective-permute-done.2.face3
  24.9 0.0 collective-permute-done.3.face4
  24.9 0.0 copy-done.2
  24.9 0.0 copy-done.3
  24.9 0.0 copy-done.6
  24.9 0.0 copy-done.10
  24.9 0.0 copy-done.11
  24.9 65.1 %patch_block.1 = (bf16[5120,128]{1,0:T(8,128)(2,1)}, f32[2048,128]{1,0:T(8,128)}) custom-call(s32[1]{0:T(128)S(6)} %copy.15.counts, s32[5]{0:T(128)S(1)} %copy-done.10, bf16[5120,128]{1,0:T(8,128)(2,1)S(1)} %get-tuple-element.20.ordered, bf16[5120,128]{1,0:T(8,128)(2,1)S(1)} %get-tuple-element.21.query, bf16[5120,128]{1,0:T(8,128)(2,1)S(1)} %get-tuple-element.22.own_keys, ...), custom_call_target="tpu_custom_call" | custom-call | tf_op jit(solution)/shard_map/patch_block/pallas_call | solution.py:304
  (3 shorter events, 0.0 us)
Async XLA Ops:
  0.6 13.0 %copy-start.9 = (f32[128]{0:T(128)S(1)}, f32[128]{0:T(128)}, u32[]{:S(2)}) copy-start(f32[128]{0:T(128)} %param.19) | copy-start | bytes 1540
  0.6 1.3 %copy-start = (bf16[5120,128]{1,0:T(8,128)(2,1)S(1)}, bf16[5120,128]{1,0:T(8,128)(2,1)}, u32[]{:S(2)}) copy-start(bf16[5120,128]{1,0:T(8,128)(2,1)} %feats.1) | copy-start | bytes 3932164
  2.0 0.7 copy-start.4
  2.7 0.8 copy-start.5
  3.5 0.7 copy-start.7
  4.2 9.5 %copy-start.1 = (bf16[128,384]{1,0:T(8,128)(2,1)S(1)}, bf16[128,384]{1,0:T(8,128)(2,1)}, u32[]{:S(2)}) copy-start(bf16[128,384]{1,0:T(8,128)(2,1)} %w_qkv.3) | copy-start | bytes 294916
  4.2 9.5 %copy-start.8 = (f32[3,256]{1,0:T(4,128)S(1)}, f32[3,256]{1,0:T(4,128)}, u32[]{:S(2)}) copy-start(f32[3,256]{1,0:T(4,128)} %pos_proj.3) | copy-start | bytes 9220
  9.2 15.7 %collective-permute-start = (bf16[1152,128]{1,0:T(8,128)(2,1)S(1)}, bf16[1152,128]{1,0:T(8,128)(2,1)S(1)}, u32[]{:S(2)}, u32[]{:S(2)}) collective-permute-start(bf16[1152,128]{1,0:T(8,128)(2,1)S(1)} %get-tuple-element.26), channel_id=1, source_target_pairs={{0,8},{8,16},{16,24},{24,32},{32,40},{40,48},{48,56},{56,64},{64,7... | collective-permute-start | bytes 884744 | tf_op jit(solution)/shard_map/ppermute | solution.py:341
  9.3 15.6 %collective-permute-start.1 = (bf16[1152,128]{1,0:T(8,128)(2,1)S(1)}, bf16[1152,128]{1,0:T(8,128)(2,1)S(1)}, u32[]{:S(2)}, u32[]{:S(2)}) collective-permute-start(bf16[1152,128]{1,0:T(8,128)(2,1)S(1)} %get-tuple-element.27), channel_id=1, source_target_pairs={{8,0},{16,8},{24,16},{32,24},{40,32},{48,40},{56,48},{64,56},{72,6... | collective-permute-start | bytes 884744 | tf_op jit(solution)/shard_map/ppermute | solution.py:341
  11.0 13.9 %collective-permute-start.2 = (bf16[1152,128]{1,0:T(8,128)(2,1)S(1)}, bf16[1152,128]{1,0:T(8,128)(2,1)S(1)}, u32[]{:S(2)}, u32[]{:S(2)}) collective-permute-start(bf16[1152,128]{1,0:T(8,128)(2,1)S(1)} %get-tuple-element.26), channel_id=1, source_target_pairs={{0,1},{1,2},{2,3},{3,4},{4,5},{5,6},{6,7},{7,0},{8,9},{9,10},{10,1... | collective-permute-start | bytes 884744 | tf_op jit(solution)/shard_map/ppermute | solution.py:341
  11.2 13.7 %collective-permute-start.3 = (bf16[1152,128]{1,0:T(8,128)(2,1)S(1)}, bf16[1152,128]{1,0:T(8,128)(2,1)S(1)}, u32[]{:S(2)}, u32[]{:S(2)}) collective-permute-start(bf16[1152,128]{1,0:T(8,128)(2,1)S(1)} %get-tuple-element.27), channel_id=1, source_target_pairs={{1,0},{2,1},{3,2},{4,3},{5,4},{6,5},{7,6},{0,7},{9,8},{10,9},{11,1... | collective-permute-start | bytes 884744 | tf_op jit(solution)/shard_map/ppermute | solution.py:341
  13.7 11.2 %copy-start.2 = (bf16[128,512]{1,0:T(8,128)(2,1)S(1)}, bf16[128,512]{1,0:T(8,128)(2,1)}, u32[]{:S(2)}) copy-start(bf16[128,512]{1,0:T(8,128)(2,1)} %w_up.1) | copy-start | bytes 393220
  13.7 11.2 %copy-start.3 = (bf16[512,128]{1,0:T(8,128)(2,1)S(1)}, bf16[512,128]{1,0:T(8,128)(2,1)}, u32[]{:S(2)}) copy-start(bf16[512,128]{1,0:T(8,128)(2,1)} %w_down.1) | copy-start | bytes 393220
  13.7 11.2 %copy-start.6 = (bf16[128,128]{1,0:T(8,128)(2,1)S(1)}, bf16[128,128]{1,0:T(8,128)(2,1)}, u32[]{:S(2)}) copy-start(bf16[128,128]{1,0:T(8,128)(2,1)} %w_out.1) | copy-start | bytes 98308
  13.7 11.2 %copy-start.10 = (s32[5]{0:T(128)S(1)}, s32[5]{0:T(128)}, u32[]{:S(2)}) copy-start(s32[5]{0:T(128)} %ghosts.1) | copy-start | bytes 64
  13.7 11.2 %copy-start.11 = (f32[128]{0:T(128)S(1)}, f32[128]{0:T(128)}, u32[]{:S(2)}) copy-start(f32[128]{0:T(128)} %param.23) | copy-start | bytes 1540
where the time goes:
time: 91.4 us; the launch traced here: 90.2 us
  Pallas kernels  79.3 us (87%)
  starting transfers between devices  3.81 us (4%)
  local copies, waits for them, and re-layouts  3.59 us (4%)
  waiting for transfers between devices  1.89 us (2%)
  between operations  1.59 us (2%)
    pallas_call x1, Pallas kernels, run_block(): pl.pallas_call(block_kernel, grid=(slots,), in_specs=[smem, smem] + [part...  65.1 us
    pallas_call x1, Pallas kernels, gather_far(): pl.pallas_call(functools.partial(far_kernel, first), in_specs=[pl.BlockSp...  9.22 us
    pallas_call x1, Pallas kernels, gather_near(): pl.pallas_call(functools.partial(near_kernel, rows), in_specs=[pl.BlockSp...  4.99 us
    ppermute x4, starting transfers between devices, ring(): return [lax.ppermute(face1, axis, up), lax.ppermute(face0, axis, down)]  3.81 us
    unnamed x24, local copies, waits for them, and re-layouts  3.59 us
    ppermute x4, waiting for transfers between devices, ring(): return [lax.ppermute(face1, axis, up), lax.ppermute(face0, axis, down)]  1.89 us
  transfers between devices with their start and end apart: 4, of which 1 were waited for; matrix products, arithmetic and copies ran while one was open for 0% of the time, Pallas kernels for 10%

commit v1 on v0

--- a/solution.py
+++ b/solution.py
@@ -1,4 +1,3 @@
-import functools
 import math
 
 import jax
@@ -12,6 +11,7 @@
 GRID = 64
 EPS = 1e-05
 CHUNK = 256
+STEP = 256
 SCALE = math.log2(math.e) / math.sqrt(32.0)
 F32 = jnp.float32
 BF16 = jnp.bfloat16
@@ -60,106 +60,187 @@
     extra[...] = dot(lines[...].astype(BF16), spot, ((0,), (0,)))
 
 
-def pick_rows(first, rows, serial, table, extra, picked, picked_extra):
-    def step(block, carry):
-        base = pl.multiple_of(block * 16, 16)
-        for r in range(16):
-            at = serial[first + base + r]
-            picked[pl.ds(base + r, 1), :] = table[pl.ds(at, 1), :]
-            picked_extra[pl.ds(base + r, 1), :] = extra[pl.ds(at, 1), :]
-        return carry
-
-    lax.fori_loop(0, rows // 16, step, 0)
-
-
-def near_kernel(rows, serial, feats, coords, cells, ordered, aux, face0, face1, table, extra, picked, picked_extra, lines):
-    build_tables(feats, coords, cells, table, extra, lines)
-    pick_rows(0, rows, serial, table, extra, picked, picked_extra)
-    ordered[...] = picked[...].astype(BF16)
-    aux[...] = picked_extra[...].astype(BF16)
+def pick_rows(serial, first, base, table, extra, rows, more):
+    for r in range(STEP):
+        at = serial[first + base + r]
+        rows[pl.ds(base + r, 1), :] = table[pl.ds(at, 1), :]
+        more[pl.ds(base + r, 1), :] = extra[pl.ds(at, 1), :]
+
+
+def make_face(face, rows, more):
+    patch = rows.shape[0]
     row = lax.broadcasted_iota(jnp.int32, (16, 128), 0)
     lane = lax.broadcasted_iota(jnp.int32, (16, 128), 1)
     pick = jnp.where((row == lane) & (row < 9), 1.0, 0.0).astype(BF16)
-    patch = rows // 2
-    for face, start in ((face0, 0), (face1, patch)):
-        face[0:patch, :] = ordered[start : start + patch, :]
-        line = dot(pick, aux[start : start + patch, :], ((1,), (1,))).astype(BF16)
-        for c in range(patch // 128):
-            face[patch + c * 16 : patch + c * 16 + 16, :] = line[:, c * 128 : c * 128 + 128]
-
-
-def far_kernel(
-    first, serial, table, extra, near, near_aux, gain1, w_qkv, pos_proj,
-    ordered, query, keys, values, side, cell_lines,
-    picked, picked_extra, w_full,
-):
-    total, width = table.shape
+    face[0:patch, :] = rows[...].astype(BF16)
+    line = dot(pick, more[...].astype(BF16), ((1,), (1,))).astype(BF16)
+    for c in range(patch // 128):
+        face[patch + c * 16 : patch + c * 16 + 16, :] = line[:, c * 128 : c * 128 + 128]
+
+
+def project_weights(w_full, w_qkv, pos_proj):
+    width = w_qkv.shape[0]
     full_weights(w_full, w_qkv, pos_proj)
     row = lax.broadcasted_iota(jnp.int32, (width, width), 0)
     w_full[0:width, 3 * width :] = jnp.zeros((width, width), BF16)
     w_full[width:, 3 * width :] = jnp.where(row == 11, 1.0, 0.0).astype(BF16)
-    pick_rows(first, total - first, serial, table, extra, picked, picked_extra)
+
+
+def project(base, offset, rows, more, gain1, w_full, outs):
+    ordered, query, keys, values, side, cell_lines = outs
+    width = rows.shape[1]
     row = lax.broadcasted_iota(jnp.int32, (8, 128), 0)
     lane = lax.broadcasted_iota(jnp.int32, (8, 128), 1)
     pick = jnp.where((row < 3) & (lane == row + 9), 1.0, 0.0).astype(BF16)
-    block = 512
-    for lower in range(0, total, block):
-        span = slice(lower, lower + block)
-        if lower < first:
-            wide = near[span, :].astype(F32)
-            aux = near_aux[span, :]
-            ordered[span, :] = near[span, :]
-        else:
-            wide = picked[lower - first : lower - first + block, :]
-            aux = picked_extra[lower - first : lower - first + block, :].astype(BF16)
-            ordered[span, :] = wide.astype(BF16)
-        normed = normed_rows(wide, gain1[...])
-        qkv = dot(jnp.concatenate([normed, aux], axis=1), w_full[...], ((1,), (0,)))
-        query[span, :] = qkv[:, :width].astype(BF16)
-        keys[span, :] = qkv[:, width : 2 * width].astype(BF16)
-        values[span, :] = qkv[:, 2 * width : 3 * width].astype(BF16)
-        side[span, :] = qkv[:, 3 * width :].astype(BF16)
-        cell_lines[:, span] = dot(pick, aux, ((1,), (1,)))
-
-
-def gather_near(serial, feats, coords, cells, rows):
+    wide = rows[pl.ds(base, STEP), :]
+    aux = more[pl.ds(base, STEP), :].astype(BF16)
+    normed = normed_rows(wide, gain1[...])
+    qkv = dot(jnp.concatenate([normed, aux], axis=1), w_full[...], ((1,), (0,)))
+    span = pl.ds(pl.multiple_of(base + offset, STEP), STEP)
+    ordered[span, :] = wide.astype(BF16)
+    query[span, :] = qkv[:, :width].astype(BF16)
+    keys[span, :] = qkv[:, width : 2 * width].astype(BF16)
+    values[span, :] = qkv[:, 2 * width : 3 * width].astype(BF16)
+    side[span, :] = qkv[:, 3 * width :].astype(BF16)
+    cell_lines[:, span] = dot(pick, aux, ((1,), (1,)))
+
+
+def steps(patch, body):
+    def step(block, carry):
+        body(pl.multiple_of(block * STEP, STEP))
+        return carry
+
+    lax.fori_loop(0, patch // STEP, step, 0)
+
+
+def first_kernel(serial_in, feats_in, coords_in, cells_in, face1, table, extra, rows1, more1, serial, feats, coords, cells, lines, sems):
+    patch = rows1.shape[0]
+    copies = [
+        pltpu.make_async_copy(feats_in, feats, sems.at[0]),
+        pltpu.make_async_copy(coords_in, coords, sems.at[1]),
+        pltpu.make_async_copy(cells_in, cells, sems.at[2]),
+        pltpu.make_async_copy(serial_in.at[pl.ds(patch, patch)], serial, sems.at[3]),
+    ]
+    for copy in copies:
+        copy.start()
+    for copy in copies:
+        copy.wait()
+    build_tables(feats, coords, cells, table, extra, lines)
+    steps(patch, lambda base: pick_rows(serial, 0, base, table, extra, rows1, more1))
+    make_face(face1, rows1, more1)
+
+
+def second_kernel(
+    serial, table, extra, rows1, more1, gain1, w_qkv, pos_proj,
+    face0, ordered, query, keys, values, side, cell_lines, rows2, more2,
+    w_full, rows0, more0,
+):
+    patch = rows1.shape[0]
+    outs = (ordered, query, keys, values, side, cell_lines)
+    project_weights(w_full, w_qkv, pos_proj)
+
+    def zero(base):
+        pick_rows(serial, 0, base, table, extra, rows0, more0)
+        project(base, patch, rows1, more1, gain1, w_full, outs)
+
+    def two(base):
+        pick_rows(serial, 2 * patch, base, table, extra, rows2, more2)
+        project(base, 0, rows0, more0, gain1, w_full, outs)
+
+    steps(patch, zero)
+    make_face(face0, rows0, more0)
+    steps(patch, two)
+
+
+def third_kernel(
+    serial, table, extra, rows2, more2, gain1, w_qkv, pos_proj,
+    near_ordered, near_query, near_keys, near_values, near_side, near_lines,
+    ordered, query, keys, values, side, cell_lines,
+    w_full, rows3, more3, rows4, more4,
+):
+    patch = rows2.shape[0]
+    outs = (ordered, query, keys, values, side, cell_lines)
+    project_weights(w_full, w_qkv, pos_proj)
+    pairs = ((ordered, near_ordered), (query, near_query), (keys, near_keys), (values, near_values), (side, near_side))
+    for far, near in pairs:
+        far[0 : 2 * patch, :] = near[...]
+    cell_lines[:, 0 : 2 * patch] = near_lines[...]
+
+    def three(base):
+        pick_rows(serial, 3 * patch, base, table, extra, rows3, more3)
+        project(base, 2 * patch, rows2, more2, gain1, w_full, outs)
+
+    def four(base):
+        pick_rows(serial, 4 * patch, base, table, extra, rows4, more4)
+        project(base, 3 * patch, rows3, more3, gain1, w_full, outs)
+
+    steps(patch, three)
+    steps(patch, four)
+    steps(patch, lambda base: project(base, 4 * patch, rows4, more4, gain1, w_full, outs))
+
+
+def gather_first(serial, feats, coords, cells, patch):
     total, width = feats.shape
-    patch = rows // 2
     vm = pl.BlockSpec(memory_space=pltpu.VMEM)
+    hbm = pl.BlockSpec(memory_space=pltpu.HBM)
     return pl.pallas_call(
-        functools.partial(near_kernel, rows),
-        in_specs=[pl.BlockSpec(memory_space=pltpu.SMEM), vm, vm, vm],
-        out_specs=[vm] * 6,
-        out_shape=[jax.ShapeDtypeStruct((rows, width), BF16), jax.ShapeDtypeStruct((rows, 128), BF16)]
-        + [jax.ShapeDtypeStruct((patch + patch // 8, width), BF16)] * 2
-        + [jax.ShapeDtypeStruct((total, width), F32), jax.ShapeDtypeStruct((total, 128), F32)],
+        first_kernel,
+        in_specs=[hbm] * 4,
+        out_specs=[vm] * 5,
+        out_shape=[
+            jax.ShapeDtypeStruct((patch + patch // 8, width), BF16),
+            jax.ShapeDtypeStruct((total, width), F32),
+            jax.ShapeDtypeStruct((total, 128), F32),
+            jax.ShapeDtypeStruct((patch, width), F32),
+            jax.ShapeDtypeStruct((patch, 128), F32),
+        ],
         scratch_shapes=[
-            pltpu.VMEM((rows, width), F32),
-            pltpu.VMEM((rows, 128), F32),
+            pltpu.SMEM((patch,), jnp.int32),
+            pltpu.VMEM(feats.shape, BF16),
+            pltpu.VMEM(coords.shape, BF16),
+            pltpu.VMEM(cells.shape, jnp.int32),
             pltpu.VMEM((8, total), F32),
+            pltpu.SemaphoreType.DMA((4,)),
         ],
         compiler_params=pltpu.CompilerParams(vmem_limit_bytes=VMEM_LIMIT),
-        name="gather_near",
-    )(serial, feats, coords, cells)
-
-
-def gather_far(serial, table, extra, near, near_aux, gain1, w_qkv, pos_proj):
-    total, width = table.shape
-    first = near.shape[0]
+        name="gather_first",
+    )(*[pltpu.with_memory_space_constraint(x, pltpu.HBM) for x in (serial, feats, coords, cells)])
+
+
+def row_shapes(rows, width):
+    return [jax.ShapeDtypeStruct((rows, width), BF16)] * 5 + [jax.ShapeDtypeStruct((8, rows), F32)]
+
+
+def gather_second(serial, table, extra, rows1, more1, gain1, w_qkv, pos_proj):
+    patch, width = rows1.shape
     vm = pl.BlockSpec(memory_space=pltpu.VMEM)
+    picked = [pltpu.VMEM((patch, width), F32), pltpu.VMEM((patch, 128), F32)]
     return pl.pallas_call(
-        functools.partial(far_kernel, first),
+        second_kernel,
         in_specs=[pl.BlockSpec(memory_space=pltpu.SMEM)] + [vm] * 7,
+        out_specs=[vm] * 9,
+        out_shape=[jax.ShapeDtypeStruct((patch + patch // 8, width), BF16)]
+        + row_shapes(2 * patch, width)
+        + [jax.ShapeDtypeStruct((patch, width), F32), jax.ShapeDtypeStruct((patch, 128), F32)],
+        scratch_shapes=[pltpu.VMEM((2 * width, 4 * width), BF16)] + picked,
+        compiler_params=pltpu.CompilerParams(vmem_limit_bytes=VMEM_LIMIT),
+        name="gather_second",
+    )(serial, table, extra, rows1, more1, gain1, w_qkv, pos_proj)
+
+
+def gather_third(serial, table, extra, rows2, more2, gain1, w_qkv, pos_proj, near):
+    patch, width = rows2.shape
+    vm = pl.BlockSpec(memory_space=pltpu.VMEM)
+    picked = [pltpu.VMEM((patch, width), F32), pltpu.VMEM((patch, 128), F32)]
+    return pl.pallas_call(
+        third_kernel,
+        in_specs=[pl.BlockSpec(memory_space=pltpu.SMEM)] + [vm] * 13,
         out_specs=[vm] * 6,
-        out_shape=[jax.ShapeDtypeStruct((total, width), BF16)] * 5 + [jax.ShapeDtypeStruct((8, total), F32)],
-        scratch_shapes=[
-            pltpu.VMEM((total - first, width), F32),
-            pltpu.VMEM((total - first, 128), F32),
-            pltpu.VMEM((2 * width, 4 * width), BF16),
-        ],
+        out_shape=row_shapes(table.shape[0], width),
+        scratch_shapes=[pltpu.VMEM((2 * width, 4 * width), BF16)] + picked * 2,
         compiler_params=pltpu.CompilerParams(vmem_limit_bytes=VMEM_LIMIT),
-        name="gather_far",
-    )(serial, table, extra, near, near_aux, gain1, w_qkv, pos_proj)
+        name="gather_third",
+    )(serial, table, extra, rows2, more2, gain1, w_qkv, pos_proj, *near)
 
 
 def block_kernel(
@@ -323,6 +404,14 @@
     )(counts, ghosts, ordered, query, own_keys, own_values, side, cell_lines, *faces, gain1, w_qkv, pos_proj, w_out, gain2, w_up, w_down)
 
 
+def send(face, shift):
+    received = []
+    for axis in ("sub", "slab"):
+        size = lax.axis_size(axis)
+        received.append(lax.ppermute(face, axis, [(i, (i + shift) % size) for i in range(size)]))
+    return received[1], received[0]
+
+
 def per_device(
     feats, coords, serial, cells, counts, ghosts, ln1_gain, w_qkv, pos_proj, w_out, ln2_gain, w_up, w_down
 ):
@@ -332,15 +421,13 @@
     sub_total = lax.axis_size("sub")
     cells2 = cells.reshape(1, rows_dev)
     gain1 = ln1_gain.reshape(1, width)
-    near, near_aux, face0, face1, table, extra = gather_near(serial, feats, coords, cells2, 2 * patch)
-    own = gather_far(serial, table, extra, near, near_aux, gain1, w_qkv, pos_proj)
-
-    def ring(axis, size):
-        up = [(i, (i + 1) % size) for i in range(size)]
-        down = [(j, i) for i, j in up]
-        return [lax.ppermute(face1, axis, up), lax.ppermute(face0, axis, down)]
-
-    faces = ring("slab", slab_total) + ring("sub", sub_total)
+    face1, table, extra, rows1, more1 = gather_first(serial, feats, coords, cells2, patch)
+    below = send(face1, 1)
+    face0, *near, rows2, more2 = gather_second(serial, table, extra, rows1, more1, gain1, w_qkv, pos_proj)
+    above = send(face0, -1)
+    own = gather_third(serial, table, extra, rows2, more2, gain1, w_qkv, pos_proj, near)
+    faces = [below[0], above[0], below[1], above[1]]
+
     planes = GRID // slab_total
     lines = GRID // sub_total
     out, pooled = run_block(

time: 91.4 us -> 94.2 us (1.031)
  the two profiles are of different devices: /device:TPU:120 before, /device:TPU:37 now
where the time goes in v1:
time: 94.2 us; the launch traced here: 94 us
  Pallas kernels  80.7 us (86%)
  starting transfers between devices  8.76 us (9%)
  waiting for transfers between devices  2.96 us (3%)
  between operations  1.62 us (2%)
    pallas_call x1, Pallas kernels, run_block(): pl.pallas_call(block_kernel, grid=(slots,), in_specs=[smem, smem] + [part...  65.3 us
    ppermute x4, starting transfers between devices, send(): lax.ppermute(face, axis, [(i, (i + shift) % size) for i in range(size)])  8.76 us
    pallas_call x1, Pallas kernels, gather_third(): pl.pallas_call(third_kernel, in_specs=[pl.BlockSpec(memory_space=pltpu.SM...  6.76 us
    pallas_call x1, Pallas kernels, gather_second(): pl.pallas_call(second_kernel, in_specs=[pl.BlockSpec(memory_space=pltpu.S...  5.14 us
    pallas_call x1, Pallas kernels, gather_first(): pl.pallas_call(first_kernel, in_specs=[hbm] * 4, out_specs=[vm] * 5, out_...  3.52 us
    ppermute x4, waiting for transfers between devices, send(): lax.ppermute(face, axis, [(i, (i + shift) % size) for i in range(size)])  2.96 us
  transfers between devices with their start and end apart: 4, of which 1 were waited for; matrix products, arithmetic and copies ran while one was open for 0% of the time, Pallas kernels for 7%

profile of v1, /device:TPU:37, one launch (start us, length us, event | category | flops | bytes accessed | tf_op | source)
XLA Modules:
  0.0 94.0 jit_solution(5001791610873723296)
XLA Ops:
  0.6 0.0 copy-start.1
  0.6 0.0 copy-start.6
  0.7 0.0 copy-start
  0.7 0.0 copy-start.4
  0.7 3.5 %gather_first.1 = (bf16[1152,128]{1,0:T(8,128)(2,1)S(1)}, f32[5120,128]{1,0:T(8,128)S(1)}, f32[5120,128]{1,0:T(8,128)S(1)}, f32[1024,128]{1,0:T(8,128)S(1)}, f32[1024,128]{1,0:T(8,128)S(1)}) custom-call(s32[5120]{0:T(1024)} %serial.3, bf16[5120,128]{1,0:T(8,128)(2,1)} %feats_in.1, bf16[3,5120]{1,0:T(4,128)(2,1)} %coords_in.1, s32[1,5120]{1,0:T(1,128)} %bitcast.8), custom_call_target="tpu_custom_call" | custom-call | tf_op jit(solution)/shard_map/gather_first/pallas_call | solution.py:186
  4.2 0.0 copy-done.1
  4.2 0.0 copy-done.6
  4.2 0.0 copy-done
  4.2 0.0 copy-done.4
  4.2 5.1 %gather_second.1 = (bf16[1152,128]{1,0:T(8,128)(2,1)S(1)}, bf16[2048,128]{1,0:T(8,128)(2,1)S(1)}, bf16[2048,128]{1,0:T(8,128)(2,1)S(1)}, bf16[2048,128]{1,0:T(8,...) custom-call(s32[5120]{0:T(1024)S(1)} %copy-done.1, ...), custom_call_target="tpu_custom_call" | custom-call | tf_op jit(solution)/shard_map/gather_second/pallas_call | solution.py:218
  9.4 0.8 collective-permute-start.1
  10.2 5.1 %collective-permute-start.3 = (bf16[1152,128]{1,0:T(8,128)(2,1)S(1)}, bf16[1152,128]{1,0:T(8,128)(2,1)S(1)}, u32[]{:S(2)}, u32[]{:S(2)}) collective-permute-start(bf16[1152,128]{1,0:T(8,128)(2,1)S(1)} %get-tuple-element.43), channel_id=1, source_target_pairs={{0,7},{1,0},{2,1},{3,2},{4,3},{5,4},{6,5},{7,6},{8,15},{9,8},{10,9... | collective-permute-start | bytes 884744 | tf_op jit(solution)/shard_map/ppermute | solution.py:411
  15.3 2.9 %collective-permute-start = (bf16[1152,128]{1,0:T(8,128)(2,1)S(1)}, bf16[1152,128]{1,0:T(8,128)(2,1)S(1)}, u32[]{:S(2)}, u32[]{:S(2)}) collective-permute-start(bf16[1152,128]{1,0:T(8,128)(2,1)S(1)} %get-tuple-element.42), channel_id=1, source_target_pairs={{0,8},{8,16},{16,24},{24,32},{32,40},{40,48},{48,56},{56,64},{64,7... | collective-permute-start | bytes 884744 | tf_op jit(solution)/shard_map/ppermute | solution.py:411
  18.1 0.0 collective-permute-start.2
  18.8 0.0 copy-start.2
  18.8 0.0 copy-start.3
  18.8 0.0 copy-start.5
  18.8 0.0 copy-start.7
  18.8 0.0 copy-start.8
  18.9 6.8 %gather_third.1 = (bf16[5120,128]{1,0:T(8,128)(2,1)S(1)}, bf16[5120,128]{1,0:T(8,128)(2,1)S(1)}, bf16[5120,128]{1,0:T(8,128)(2,1)S(1)}, bf16[5120,128]{1,0:T(8,1...) custom-call(s32[5120]{0:T(1024)S(1)} %copy-done.1, f32[5120,128]{1,0:T(8,128)S(1)} %get-tuple-element.24.table, ...), custom_call_target="tpu_custom_call" | custom-call | tf_op jit(solution)/shard_map/gather_third/pallas_call | solution.py:235
  25.6 0.0 collective-permute-done.1.face2
  25.6 0.0 collective-permute-done.3.face4
  25.6 0.0 collective-permute-done.face1
  25.7 2.9 %collective-permute-done.2.face3 = bf16[1152,128]{1,0:T(8,128)(2,1)S(1)} collective-permute-done((bf16[1152,128]{1,0:T(8,128)(2,1)S(1)}, bf16[1152,128]{1,0:T(8,128)(2,1)S(1)}, u32[]{:S(2)}, u32[]{:S(2)}) %collective-permute-start.2) | collective-permute-done | bytes 294944 | tf_op jit(solution)/shard_map/ppermute | solution.py:411
  28.6 0.0 copy-done.2
  28.6 0.0 copy-done.3
  28.6 0.0 copy-done.5
  28.6 0.0 copy-done.7
  28.6 0.0 copy-done.8
  28.6 65.3 %patch_block.1 = (bf16[5120,128]{1,0:T(8,128)(2,1)}, f32[2048,128]{1,0:T(8,128)}) custom-call(s32[1]{0:T(128)S(6)} %copy.15.counts, s32[5]{0:T(128)S(1)} %copy-done.7, bf16[5120,128]{1,0:T(8,128)(2,1)S(1)} %get-tuple-element.36.ordered, bf16[5120,128]{1,0:T(8,128)(2,1)S(1)} %get-tuple-element.37.query, bf16[5120,128]{1,0:T(8,128)(2,1)S(1)} %get-tuple-element.38.own_keys, ...), custom_call_target="tpu_custom_call" | custom-call | tf_op jit(solution)/shard_map/patch_block/pallas_call | solution.py:385
Async XLA Ops:
  0.6 3.6 %copy-start.1 = (s32[5120]{0:T(1024)S(1)}, s32[5120]{0:T(1024)}, u32[]{:S(2)}) copy-start(s32[5120]{0:T(1024)} %serial.3) | copy-start | bytes 61444
  0.6 3.6 %copy-start.6 = (f32[128]{0:T(128)S(1)}, f32[128]{0:T(128)}, u32[]{:S(2)}) copy-start(f32[128]{0:T(128)} %param.19) | copy-start | bytes 1540
  0.7 3.6 %copy-start = (bf16[128,384]{1,0:T(8,128)(2,1)S(1)}, bf16[128,384]{1,0:T(8,128)(2,1)}, u32[]{:S(2)}) copy-start(bf16[128,384]{1,0:T(8,128)(2,1)} %w_qkv.5) | copy-start | bytes 294916
  0.7 3.6 %copy-start.4 = (f32[3,256]{1,0:T(4,128)S(1)}, f32[3,256]{1,0:T(4,128)}, u32[]{:S(2)}) copy-start(f32[3,256]{1,0:T(4,128)} %pos_proj.5) | copy-start | bytes 9220
  9.4 16.2 %collective-permute-start.1 = (bf16[1152,128]{1,0:T(8,128)(2,1)S(1)}, bf16[1152,128]{1,0:T(8,128)(2,1)S(1)}, u32[]{:S(2)}, u32[]{:S(2)}) collective-permute-start(bf16[1152,128]{1,0:T(8,128)(2,1)S(1)} %get-tuple-element.43), channel_id=1, source_target_pairs={{0,120},{8,0},{16,8},{24,16},{32,24},{40,32},{48,40},{56,48},{64,5... | collective-permute-start | bytes 884744 | tf_op jit(solution)/shard_map/ppermute | solution.py:411
  10.2 15.5 %collective-permute-start.3 = (bf16[1152,128]{1,0:T(8,128)(2,1)S(1)}, bf16[1152,128]{1,0:T(8,128)(2,1)S(1)}, u32[]{:S(2)}, u32[]{:S(2)}) collective-permute-start(bf16[1152,128]{1,0:T(8,128)(2,1)S(1)} %get-tuple-element.43), channel_id=1, source_target_pairs={{0,7},{1,0},{2,1},{3,2},{4,3},{5,4},{6,5},{7,6},{8,15},{9,8},{10,9... | collective-permute-start | bytes 884744 | tf_op jit(solution)/shard_map/ppermute | solution.py:411
  15.3 10.4 %collective-permute-start = (bf16[1152,128]{1,0:T(8,128)(2,1)S(1)}, bf16[1152,128]{1,0:T(8,128)(2,1)S(1)}, u32[]{:S(2)}, u32[]{:S(2)}) collective-permute-start(bf16[1152,128]{1,0:T(8,128)(2,1)S(1)} %get-tuple-element.42), channel_id=1, source_target_pairs={{0,8},{8,16},{16,24},{24,32},{32,40},{40,48},{48,56},{56,64},{64,7... | collective-permute-start | bytes 884744 | tf_op jit(solution)/shard_map/ppermute | solution.py:411
  18.1 10.5 %collective-permute-start.2 = (bf16[1152,128]{1,0:T(8,128)(2,1)S(1)}, bf16[1152,128]{1,0:T(8,128)(2,1)S(1)}, u32[]{:S(2)}, u32[]{:S(2)}) collective-permute-start(bf16[1152,128]{1,0:T(8,128)(2,1)S(1)} %get-tuple-element.42), channel_id=1, source_target_pairs={{0,1},{1,2},{2,3},{3,4},{4,5},{5,6},{6,7},{7,0},{8,9},{9,10},{10,1... | collective-permute-start | bytes 884744 | tf_op jit(solution)/shard_map/ppermute | solution.py:411
  18.8 9.8 %copy-start.2 = (bf16[128,512]{1,0:T(8,128)(2,1)S(1)}, bf16[128,512]{1,0:T(8,128)(2,1)}, u32[]{:S(2)}) copy-start(bf16[128,512]{1,0:T(8,128)(2,1)} %w_up.1) | copy-start | bytes 393220
  18.8 9.8 %copy-start.3 = (bf16[512,128]{1,0:T(8,128)(2,1)S(1)}, bf16[512,128]{1,0:T(8,128)(2,1)}, u32[]{:S(2)}) copy-start(bf16[512,128]{1,0:T(8,128)(2,1)} %w_down.1) | copy-start | bytes 393220
  18.8 9.8 %copy-start.5 = (bf16[128,128]{1,0:T(8,128)(2,1)S(1)}, bf16[128,128]{1,0:T(8,128)(2,1)}, u32[]{:S(2)}) copy-start(bf16[128,128]{1,0:T(8,128)(2,1)} %w_out.1) | copy-start | bytes 98308
  18.8 9.8 %copy-start.7 = (s32[5]{0:T(128)S(1)}, s32[5]{0:T(128)}, u32[]{:S(2)}) copy-start(s32[5]{0:T(128)} %ghosts.1) | copy-start | bytes 64
  18.8 9.8 %copy-start.8 = (f32[128]{0:T(128)S(1)}, f32[128]{0:T(128)}, u32[]{:S(2)}) copy-start(f32[128]{0:T(128)} %param.23) | copy-start | bytes 1540
